TPU v7x, 256 devices: a whole 4x4x8 slice. The times are simulated.
256 devices in a mesh: row: 8 (over y, core), col: 32 (over z, x).
Axes of the slice: x: 4, y: 4, z: 8, core: 2. Of those that a mesh axis runs over, the one named last changes fastest.
Arguments:
- band: float32 [4, 8, 1, 32, 512, 512], P(None, 'row', None, 'col'), as said below
Outputs:
- factored: float32 [4, 8, 1, 32, 512, 512], P(None, 'row', None, 'col')
Inputs may be any that keep to these rules, and one draw needn't show every extreme that they name: band holds the tiles of a symmetric matrix; its diagonal tiles are symmetric positive definite, and those of tile columns 0 and 1 leave every pivot of the steps positive.
All inputs are finite; a program needn't handle non-finite values.
Results may differ from a plain program's by a relative error of at most 0.00015.
Values sent between devices are 32-bit elements; how exact they have to be, the bound alone decides.
No kernel may reach another device: no remote copies, remote signals or barrier semaphores. Data moves between devices by JAX's collectives and lax.ppermute only.
A program may use at most 128 MiB of HBM per device.

v0:
```python
import jax
import jax.numpy as jnp
from jax import lax
from jax.experimental import pallas as pl
from jax.experimental.pallas import tpu as pltpu
from jax.sharding import PartitionSpec as P


TILE = 512
NB = 128
NBLK = TILE // NB
PART = TILE // 8
HIGHEST = lax.Precision.HIGHEST
VMEM = pl.BlockSpec(memory_space=pltpu.VMEM)
SMEM = pl.BlockSpec(memory_space=pltpu.SMEM)
F32 = jnp.float32


def square(n=1):
    return (jax.ShapeDtypeStruct((TILE, TILE), F32),) * n


def times_t(a, b):
    return lax.dot_general(a, b, (((1,), (1,)), ((), ())), precision=HIGHEST, preferred_element_type=F32)


def block_factor(s):
    rows = lax.broadcasted_iota(jnp.int32, (8, NB), 0)
    cols = lax.broadcasted_iota(jnp.int32, (8, NB), 1)

    def lane(v, c):
        return jnp.broadcast_to(v[:, c : c + 1], (8, NB))

    def sub(v, j):
        return jnp.broadcast_to(v[j : j + 1, :], (8, NB))

    upper, inverse = [None] * 16, [None] * 16
    for g in range(16):
        o = 8 * g
        inside = (cols >= o) & (cols < o + 8)
        c = [lane(s[g], o + k) for k in range(8)]
        s[g] = jnp.where(inside, jnp.where(cols == rows + o, 1.0, 0.0), s[g])
        inv, q, sr = [None] * 8, [[None] * 8 for _ in range(8)], [None] * 8
        pivots = None
        for k in range(8):
            piv = sub(c[k], k)
            pivots = piv if k == 0 else jnp.where(rows == k, piv, pivots)
            inv[k] = 1.0 / piv
            sr[k] = sub(s[g], k)
            if k < 7:
                t = jnp.where(rows > k, c[k] * inv[k], 0.0)
                for k2 in range(k + 1, 8):
                    q[k][k2] = sub(c[k2], k)
                    c[k2] = c[k2] - t * q[k][k2]
                s[g] = s[g] - t * sr[k]
        for i in range(g + 1, 16):
            ci = [lane(s[i], o + k) for k in range(8)]
            s[i] = jnp.where(inside, 0.0, s[i])
            for k in range(8):
                t = ci[k] * inv[k]
                for k2 in range(k + 1, 8):
                    ci[k2] = ci[k2] - t * q[k][k2]
                s[i] = s[i] - t * sr[k]
        block = s[g]
        for k in range(8):
            block = jnp.where(cols == o + k, c[k], block)
        r = lax.rsqrt(pivots)
        upper[g] = jnp.where(cols >= rows + o, block * r, 0.0)
        inverse[g] = jnp.where(cols <= rows + o, s[g] * r, 0.0)
    return jnp.concatenate(upper, 0), jnp.concatenate(inverse, 0)


def factor_tile(w_ref, l_ref, v_ref):
    v_ref[...] = jnp.zeros((TILE, TILE), F32)
    l_ref[...] = jnp.zeros((TILE, TILE), F32)

    def step(b, carry):
        off = pl.multiple_of(b * NB, NB)
        ub, vb = block_factor([w_ref[pl.ds(off + 8 * i, 8), pl.ds(off, NB)] for i in range(16)])
        lb = ub.T
        for bb in range(NBLK):

            @pl.when(b == bb)
            def _(bb=bb):
                o = bb * NB
                e = o + NB
                l_ref[o:e, o:e] = lb
                if bb > 0:
                    v_ref[o:e, :o] = jnp.dot(vb, v_ref[o:e, :o], precision=HIGHEST, preferred_element_type=F32)
                v_ref[o:e, o:e] = vb
                if bb < NBLK - 1:
                    lp = times_t(w_ref[e:, o:e], vb)
                    l_ref[e:, o:e] = lp
                    w_ref[e:, e:] -= times_t(lp, lp)
                    v_ref[e:, :e] -= jnp.dot(lp, v_ref[o:e, :e], precision=HIGHEST, preferred_element_type=F32)

        return carry

    lax.fori_loop(0, NBLK, step, 0)


def assemble(dst_ref, mine_ref, other_ref, t, where_ref):
    y, core = where_ref[0], where_ref[1]
    for m in range(4):
        at = lax.rem(y + 4 - m, 4) * 2
        for src, k in ((mine_ref, core), (other_ref, 1 - core)):
            dst_ref[pl.ds(pl.multiple_of((at + k) * PART, PART), PART), :] = src[m, t]


def first_kernel(where_ref, mine_ref, other_ref, l_ref, v_ref, w_ref):
    assemble(w_ref, mine_ref, other_ref, 0, where_ref)
    factor_tile(w_ref, l_ref, v_ref)


def factor_first(where, mine, other):
    return pl.pallas_call(
        first_kernel,
        out_shape=square(2),
        in_specs=[SMEM, VMEM, VMEM],
        out_specs=(VMEM,) * 2,
        scratch_shapes=[pltpu.VMEM((TILE, TILE), F32)],
        cost_estimate=pl.CostEstimate(flops=10**10, bytes_accessed=3 << 20, transcendentals=0),
        name="factor_first",
    )(where, mine, other)


def second_kernel(where_ref, mine_ref, other_ref, v0_ref, p_ref, l_ref, v_ref, w_ref):
    assemble(w_ref, mine_ref, other_ref, 0, where_ref)
    p_ref[...] = times_t(w_ref[...], v0_ref[...])
    assemble(w_ref, mine_ref, other_ref, 1, where_ref)
    w_ref[...] -= times_t(p_ref[...], p_ref[...])
    factor_tile(w_ref, l_ref, v_ref)


def factor_second(where, mine, other, inverse0):
    return pl.pallas_call(
        second_kernel,
        out_shape=square(3),
        in_specs=[SMEM, VMEM, VMEM, VMEM],
        out_specs=(VMEM,) * 3,
        scratch_shapes=[pltpu.VMEM((TILE, TILE), F32)],
        cost_estimate=pl.CostEstimate(flops=10**10, bytes_accessed=6 << 20, transcendentals=0),
        name="factor_second",
    )(where, mine, other, inverse0)


def split(v):
    hi = v.astype(jnp.bfloat16)
    return hi, (v - hi.astype(F32)).astype(jnp.bfloat16)


def times_t3(a, b):
    def one(p, q):
        return lax.dot_general(p, q, (((1,), (1,)), ((), ())), preferred_element_type=F32)

    return one(a[0], b[0]) + (one(a[0], b[1]) + one(a[1], b[0]))


def prepare_kernel(where_ref, mine_ref, other_ref, v0_ref, p01_ref, v1_ref, p0_ref, p1_ref, w_ref):
    assemble(w_ref, mine_ref, other_ref, 2, where_ref)
    p0 = times_t3(split(w_ref[...]), split(v0_ref[...]))
    p0_ref[...] = p0
    assemble(w_ref, mine_ref, other_ref, 3, where_ref)
    next1 = w_ref[...] - times_t3(split(p0), split(p01_ref[...]))
    p1_ref[...] = times_t3(split(next1), split(v1_ref[...]))


def prepare(where, mine, other, inverse0, p01, inverse1):
    return pl.pallas_call(
        prepare_kernel,
        out_shape=square(2),
        in_specs=[SMEM] + [VMEM] * 5,
        out_specs=(VMEM,) * 2,
        scratch_shapes=[pltpu.VMEM((TILE, TILE), F32)],
        cost_estimate=pl.CostEstimate(flops=3 * 10**9, bytes_accessed=9 << 20, transcendentals=0),
        name="prepare",
    )(where, mine, other, inverse0, p01, inverse1)


UPDATE_BOTH, UPDATE_SECOND, KEEP, PANEL0, PANEL1, LATE_PANEL1, FACTOR0, FACTOR1 = range(8)


HALF = TILE // 2


def finish_kernel(at_ref, kind_ref, raw_ref, a_ref, v0, p01, v1, p0j, p1j, f0, f1, o_ref, w_ref):
    kind = kind_ref[pl.program_id(0)]

    @pl.when((pl.program_id(0) == 0) & (pl.program_id(1) == 0))
    def _():
        for n, ref in enumerate((v0, p01, v1, p0j, p1j)):
            hi, lo = split(ref[...])
            w_ref[n] = jnp.concatenate([hi, lo, hi], 1)

    def times(v, n):
        hi, lo = split(v)
        return lax.dot_general(
            jnp.concatenate([hi, hi, lo], 1), w_ref[n], (((1,), (1,)), ((), ())), preferred_element_type=F32
        )

    def raw(t):
        return raw_ref[:, t].reshape(HALF, TILE)

    @pl.when(kind == UPDATE_BOTH)
    def _():
        p0 = times(raw(0), 0)
        p1 = times(raw(1) - times(p0, 1), 2)
        o_ref[0] = a_ref[0] - times(p0, 3) - times(p1, 4)

    @pl.when(kind == UPDATE_SECOND)
    def _():
        o_ref[0] = a_ref[0] - times(times(raw(1), 2), 4)

    @pl.when(kind == PANEL0)
    def _():
        o_ref[0] = times(raw(0), 0)

    @pl.when(kind == PANEL1)
    def _():
        p0 = times(raw(0), 0)
        o_ref[0] = times(raw(1) - times(p0, 1), 2)

    @pl.when(kind == LATE_PANEL1)
    def _():
        o_ref[0] = times(raw(1), 2)

    @pl.when(kind == KEEP)
    def _():
        o_ref[...] = a_ref[...]

    @pl.when(kind == FACTOR0)
    def _():
        o_ref[0] = f0[...]

    @pl.when(kind == FACTOR1)
    def _():
        o_ref[0] = f1[...]


def finish(at, kind, panels, local, inverse0, p01, inverse1, p0j, p1j, factor0, factor1):
    whole = pl.BlockSpec((TILE, TILE), lambda s, h, at, kind: (0, 0))
    tile = pl.BlockSpec((1, HALF, TILE), lambda s, h, at, kind: (s, h, 0))
    half = pl.BlockSpec((HALF, TILE), lambda s, h, at, kind: (h, 0))
    return pl.pallas_call(
        finish_kernel,
        out_shape=jax.ShapeDtypeStruct(local.shape, F32),
        grid_spec=pltpu.PrefetchScalarGridSpec(
            num_scalar_prefetch=2,
            grid=(local.shape[0], 2),
            in_specs=[pl.BlockSpec((4, 2, PART, TILE), lambda s, h, at, kind: (2 * at[s] + h, 0, 0, 0)), tile]
            + [whole] * 5
            + [half] * 2,
            out_specs=tile,
            scratch_shapes=[pltpu.VMEM((5, TILE, 3 * TILE), jnp.bfloat16)],
        ),
        cost_estimate=pl.CostEstimate(flops=3 * 10**10, bytes_accessed=24 << 20, transcendentals=0),
        name="finish",
    )(at, kind, panels, local, inverse0, p01, inverse1, p0j, p1j, factor0, factor1)


BANDT = 32
ROWS = 8
COLS = 32
AX = ("row", "col")


def lin(r, c):
    return (r % ROWS) * COLS + c % COLS


def zx(z, x):
    return (z % 8) * 4 + x % 4


def permute(v, pairs):
    return lax.ppermute(v, AX, [(lin(*a), lin(*b)) for a, b in pairs])


EVERY = [(r, z, x) for r in range(ROWS) for z in range(8) for x in range(4)]


def core_swap(v):
    return permute(v, [((r, zx(z, x)), (r ^ 1, zx(z, x))) for r, z, x in EVERY])


def y_shift(v, k):
    return permute(v, [((r, zx(z, x)), (r + 2 * k, zx(z, x))) for r, z, x in EVERY])


def x_deal(v, k):
    return permute(v, [((r, zx(z, x)), (r, zx(z, x + k))) for r, z, x in EVERY if x < 2])


def z_deal(v, k):
    return permute(v, [((r, zx(0, x)), (r, zx(k, x))) for r, z, x in EVERY if z == 0 and x < 2])


def pick(choices):
    total = None
    for cond, v in choices:
        v = jnp.where(cond, v, 0.0)
        total = v if total is None else total + v
    return total


def spread_x(v, x):
    got = permute(v, [((r, zx(0, 0)), (r, zx(0, 2))) for r in range(ROWS)])
    v = jnp.where(x == 2, got, v)
    got = permute(v, [((r, zx(0, a)), (r, zx(0, a + 1))) for r in range(ROWS) for a in (0, 2)])
    return jnp.where(x % 2 == 1, got, v)


def spread_z(v, z, steps):
    for step in steps:
        pairs = [((r, zx(a, b)), (r, zx(a + step, b))) for r in range(ROWS) for a in range(0, 8, 2 * step) for b in range(4)]
        got = permute(v, pairs)
        v = jnp.where(z % (2 * step) == step, got, v)
    return v


def ring(piece):
    return [piece] + [y_shift(piece, m) for m in range(1, 4)]


def with_partner(pieces):
    mine = jnp.stack(pieces)
    return mine, core_swap(mine)


def shards(band):
    slots, _, _, _, tile, _ = band.shape
    part = tile // ROWS
    row = lax.axis_index("row")
    col = lax.axis_index("col")
    z, x = col // 4, col % 4
    y, core = row // 2, row % 2
    local = band.reshape(slots, tile, tile)
    where = jnp.stack([y, core]).astype(jnp.int32)

    eighths = local.reshape(8, slots * tile // 8, tile)
    skip = jnp.where((row == 0) & (x == 1), 6, 0)

    def eighth(k):
        return lax.dynamic_index_in_dim(eighths, (skip + k) % 8, 0, keepdims=False)

    arrived = [z_deal(eighth(k), k) for k in range(1, 8)]

    partner = core_swap(local[0])
    even = jnp.where(core == 0, local[0], partner).reshape(4, 2, part, tile)
    odd = jnp.where(core == 0, partner, local[0]).reshape(4, 2, part, tile)
    both = jnp.stack([even, odd], 1)
    both = lax.dynamic_index_in_dim(both, core, 2, keepdims=False)
    mine = [(y == 0, both[0])] + [(y == k, y_shift(both[k], k)) for k in range(1, 4)]
    mine = pick(mine)
    first = spread_z(spread_x(mine[:1], x), z, (4,))
    beside = permute(mine[1], [((r, 1), (r, 0)) for r in range(ROWS)])
    second = spread_x(jnp.stack([mine[1], beside]), x)
    first, second, arrived = lax.optimization_barrier((first, second, arrived))
    first, second = spread_z(first, z, (2, 1)), spread_z(second, z, (4, 2, 1))
    first = with_partner(ring(first))

    dealt = pick([(z == 0, eighth(0))] + [(z == k, arrived[k - 1]) for k in range(1, 8)])
    fourths = dealt.reshape(4, part, tile)
    p0, p1 = [(x == 0, fourths[0])], [(x == 1, fourths[1])]
    for k in range(1, 4):
        got = x_deal(jnp.where(x == 0, fourths[k], fourths[(k + 1) % 4]), k)
        p0.append((x == k, got))
        p1.append((x == (k + 1) % 4, got))
    piece = jnp.stack([pick(p0), pick(p1)])
    panels = lax.all_gather(piece, "col")

    pairs = [((r, 8 * s + q), (q, 8 * s + r)) for s in range(slots) for r in range(ROWS) for q in range(ROWS)]
    rest = ring(jnp.concatenate([second, permute(piece, pairs)]))
    factor0, inverse0 = factor_first(where, *first)
    inverse0, rest = lax.optimization_barrier((inverse0, rest))
    rest = with_partner(rest)
    p01, factor1, inverse1 = factor_second(where, *rest, inverse0)
    p0j, p1j = prepare(where, *rest, inverse0, p01, inverse1)

    rows_here = col + (row - col) % ROWS + ROWS * jnp.arange(slots, dtype=jnp.int32)
    at = (rows_here // ROWS) % slots
    update = jnp.where(rows_here < BANDT, UPDATE_BOTH, jnp.where(rows_here == BANDT, UPDATE_SECOND, KEEP))
    panel0 = jnp.where(rows_here == 0, FACTOR0, PANEL0)
    panel1 = jnp.where(rows_here == 1, FACTOR1, jnp.where(rows_here == BANDT, LATE_PANEL1, PANEL1))
    kind = jnp.where(col == 0, panel0, jnp.where(col == 1, panel1, update)).astype(jnp.int32)
    out = finish(at, kind, panels, local, inverse0, p01, inverse1, p0j, p1j, factor0, factor1)
    return out.reshape(band.shape)


def solution(mesh):
    spec = P(None, "row", None, "col", None, None)

    return jax.shard_map(shards, mesh=mesh, in_specs=(spec,), out_specs=spec, check_vma=False)
```

profile of v0, /device:TPU:57, one launch (start us, length us, event | category | flops | bytes accessed | tf_op | source)
XLA Modules:
  0.0 257.8 jit_solution(16022043125295048310)
XLA Ops:
  8.6 2.3 collective-permute-done
  12.6 2.2 collective-permute-start.2
  14.8 5.2 %collective-permute-done.1 = f32[2,64,512]{2,1,0:T(8,128)S(1)} collective-permute-done((f32[2,64,512]{2,1,0:T(8,128)S(1)}, f32[2,64,512]{2,1,0:T(8,128)S(1)}, u32[]{:S(2)}, u32[]{:S(2)}) %collective-permute-start.1) | collective-permute-done | bytes 262176 | tf_op jit(solution)/shard_map/ppermute | solution.py:276
  20.1 1.5 collective-permute-done.2
  21.6 6.4 %collective-permute-done.3 = f32[2,64,512]{2,1,0:T(8,128)S(1)} collective-permute-done((f32[2,64,512]{2,1,0:T(8,128)S(1)}, f32[2,64,512]{2,1,0:T(8,128)S(1)}, u32[]{:S(2)}, u32[]{:S(2)}) %collective-permute-start.3) | collective-permute-done | bytes 262176 | tf_op jit(solution)/shard_map/ppermute | solution.py:276
  30.4 3.7 %dynamic-slice_bitcast_fusion = (f32[256,512]{1,0:T(8,128)S(1)}, f32[256,512]{1,0:T(8,128)S(1)}, f32[256,512]{1,0:T(8,128)S(1)}, f32[256,512]{1,0:T(8,128)S(1)},...) fusion(f32[8,256,512]{2,1,0:T(8,128)} %bitcast.73, s32[]{:T(128)S(6)} %select_n.432, ...), kind=kLoop, calls=%fused_computation.14 | loop fusion | bytes 7340060 | tf_op jit(solution)/shard_map/jit(dynamic_index_in_dim)/squeeze | solution.py:344
  35.3 1.5 collective-permute-start.11
  40.4 16.8 %collective-permute-done.10 = f32[256,512]{1,0:T(8,128)} collective-permute-done((f32[256,512]{1,0:T(8,128)}, f32[256,512]{1,0:T(8,128)}, u32[]{:S(2)}, u32[]{:S(2)}) %collective-permute-start.10) | collective-permute-done | bytes 524320 | tf_op jit(solution)/shard_map/ppermute | solution.py:276
  63.9 1.8 fusion.6
  65.7 2.1 collective-permute-start.17
  69.1 1.9 collective-permute-start.19
  71.1 3.7 %collective-permute-done.19 = f32[64,512]{1,0:T(8,128)S(1)} collective-permute-done((f32[64,512]{1,0:T(8,128)S(1)}, f32[64,512]{1,0:T(8,128)S(1)}, u32[]{:S(2)}, u32[]{:S(2)}) %collective-permute-start.19) | collective-permute-done | bytes 131104 | tf_op jit(solution)/shard_map/ppermute | solution.py:276
  79.3 41.4 %collective-permute-done.21 = f32[1,64,512]{2,1,0:T(8,128)S(1)} collective-permute-done((f32[1,64,512]{2,1,0:T(8,128)S(1)}, f32[1,64,512]{2,1,0:T(8,128)S(1)}, u32[]{:S(2)}, u32[]{:S(2)}) %collective-permute-start.21) | collective-permute-done | bytes 131104 | tf_op jit(solution)/shard_map/ppermute | solution.py:276
  124.5 1.7 collective-permute-done.23
  127.6 11.7 %collective-permute-start.25 = (f32[4,1,64,512]{3,2,1,0:T(8,128)S(1)}, f32[4,1,64,512]{3,2,1,0:T(8,128)}, u32[]{:S(2)}, u32[]{:S(2)}) collective-permute-start(f32[4,1,64,512]{3,2,1,0:T(8,128)S(1)} %pad_maximum_fusion.1.mine_ref), channel_id=1, source_target_pairs={{0,32},{1,33},{2,34},{3,35},{4,36},{5,37},{6,38},{7,39},{8,40},{9,... | collective-permute-start | bytes 1572872 | tf_op jit(solution)/shard_map/ppermute | solution.py:276
  139.3 2.9 %collective-permute-start.29 = (f32[2,64,512]{2,1,0:T(8,128)S(1)}, f32[2,64,512]{2,1,0:T(8,128)S(1)}, u32[]{:S(2)}, u32[]{:S(2)}) collective-permute-start(f32[2,64,512]{2,1,0:T(8,128)S(1)} %copy-done.1), channel_id=1, source_target_pairs={{0,0},{1,32},{2,64},{3,96},{4,128},{5,160},{6,192},{7,224},{32,1},... | collective-permute-start | bytes 786440 | tf_op jit(solution)/shard_map/ppermute | solution.py:276
  142.9 14.5 %collective-permute-done.29 = f32[2,64,512]{2,1,0:T(8,128)S(1)} collective-permute-done((f32[2,64,512]{2,1,0:T(8,128)S(1)}, f32[2,64,512]{2,1,0:T(8,128)S(1)}, u32[]{:S(2)}, u32[]{:S(2)}) %collective-permute-start.29) | collective-permute-done | bytes 262176 | tf_op jit(solution)/shard_map/ppermute | solution.py:276
  158.9 21.7 %factor_first.1 = (f32[512,512]{1,0:T(8,128)}, f32[512,512]{1,0:T(8,128)}) custom-call(s32[2]{0:T(128)} %pad_add_fusion.where_ref, f32[4,1,64,512]{3,2,1,0:T(8,128)} %copy-done.2, f32[4,1,64,512]{3,2,1,0:T(8,128)} %collective-permute-done.25.other_ref), custom_call_target="tpu_custom_call" | custom-call | flops 10000000000 | bytes 3145728 | tf_op jit(solution)/shard_map/factor_first/pallas_call | solution.py:116
  180.7 3.7 %collective-permute-done.32 = f32[4,64,512]{2,1,0:T(8,128)S(1)} collective-permute-done((f32[4,64,512]{2,1,0:T(8,128)S(1)}, f32[4,64,512]{2,1,0:T(8,128)S(1)}, u32[]{:S(2)}, u32[]{:S(2)}) %collective-permute-start.32) | collective-permute-done | bytes 524320 | tf_op jit(solution)/shard_map/ppermute | solution.py:276
  185.1 1.5 pad_maximum_fusion.mine_ref
  188.4 2.8 %collective-permute-done.33.other_ref = f32[4,4,64,512]{3,2,1,0:T(8,128)} collective-permute-done((f32[4,4,64,512]{3,2,1,0:T(8,128)S(1)}, f32[4,4,64,512]{3,2,1,0:T(8,128)}, u32[]{:S(2)}, u32[]{:S(2)}) %collective-permute-start.33) | collective-permute-done | bytes 2097184 | tf_op jit(solution)/shard_map/ppermute | solution.py:276
  191.2 27.0 %factor_second.1 = (f32[512,512]{1,0:T(8,128)}, f32[512,512]{1,0:T(8,128)}, f32[512,512]{1,0:T(8,128)}) custom-call(s32[2]{0:T(128)} %pad_add_fusion.where_ref, f32[4,4,64,512]{3,2,1,0:T(8,128)} %copy-done, f32[4,4,64,512]{3,2,1,0:T(8,128)} %collective-permute-done.33.other_ref, f32[512,512]{1,0:T(8,128)} %get-tuple-element.36.v0_ref.v0), custom_call_target="tpu_custom_call" | custom-call | flops 10000000000 | bytes 6291456 | tf_op jit(solution)/shard_map/factor_second/pallas_call | solution.py:136
  218.2 6.8 %prepare.1 = (f32[512,512]{1,0:T(8,128)}, f32[512,512]{1,0:T(8,128)}) custom-call(s32[2]{0:T(128)} %pad_add_fusion.where_ref, f32[4,4,64,512]{3,2,1,0:T(8,128)} %copy-done, f32[4,4,64,512]{3,2,1,0:T(8,128)} %collective-permute-done.33.other_ref, f32[512,512]{1,0:T(8,128)} %get-tuple-element.36.v0_ref.v0, f32[512,512]{1,0:T(8,128)} %get-tuple-element.41.p01_ref.p01, ...), custom_call_target="tpu_custom_call" | custom-call | flops 3000000000 | bytes 9437184 | tf_op jit(solution)/shard_map/prepare/pallas_call | solution.py:169
  225.0 26.0 %finish.1 = f32[4,512,512]{2,1,0:T(8,128)} custom-call(s32[4]{0:T(128)} %and_select_fusion.at_ref, s32[4]{0:T(128)} %broadcast_select_fusion.13.kind_ref, f32[32,2,64,512]{3,2,1,0:T(8,128)} %bitcast.89, f32[4,512,512]{2,1,0:T(8,128)} %bitcast.75, f32[512,512]{1,0:T(8,128)} %get-tuple-element.36.v0_ref.v0, f32[512,512]{1,0:T(8,128)} %get-tuple-element.41.p01_ref.p01, ...), custom_call_target="tpu_custom_call" | custom-call | flops 30000001024 | bytes 25165824 | tf_op jit(solution)/shard_map/finish/pallas_call | solution.py:244
  (91 shorter events, 33.2 us)
Async XLA Ops:
  6.5 218.4 %all-gather.3.cloned.1.call-start = ((), (), s32[]{:S(2)}) async-start(), calls=%async_computation | async-start | bytes 8650752 | tf_op jit(solution)/shard_map/all_gather | solution.py:370
  12.5 7.6 %collective-permute-start.1 = (f32[2,64,512]{2,1,0:T(8,128)S(1)}, f32[2,64,512]{2,1,0:T(8,128)S(1)}, u32[]{:S(2)}, u32[]{:S(2)}) collective-permute-start(f32[2,64,512]{2,1,0:T(8,128)S(1)} %get-tuple-element.56), channel_id=1, source_target_pairs={{0,64},{1,65},{2,66},{3,67},{4,68},{5,69},{6,70},{7,71},{8,72},{9,... | collective-permute-start | bytes 786440 | tf_op jit(solution)/shard_map/ppermute | solution.py:276
  12.6 9.0 %collective-permute-start.2 = (f32[2,64,512]{2,1,0:T(8,128)S(1)}, f32[2,64,512]{2,1,0:T(8,128)S(1)}, u32[]{:S(2)}, u32[]{:S(2)}) collective-permute-start(f32[2,64,512]{2,1,0:T(8,128)S(1)} %get-tuple-element.57), channel_id=1, source_target_pairs={{0,128},{1,129},{2,130},{3,131},{4,132},{5,133},{6,134},{7,135},{8... | collective-permute-start | bytes 786440 | tf_op jit(solution)/shard_map/ppermute | solution.py:276
  14.8 13.2 %collective-permute-start.3 = (f32[2,64,512]{2,1,0:T(8,128)S(1)}, f32[2,64,512]{2,1,0:T(8,128)S(1)}, u32[]{:S(2)}, u32[]{:S(2)}) collective-permute-start(f32[2,64,512]{2,1,0:T(8,128)S(1)} %get-tuple-element.58), channel_id=1, source_target_pairs={{0,192},{1,193},{2,194},{3,195},{4,196},{5,197},{6,198},{7,199},{8... | collective-permute-start | bytes 786440 | tf_op jit(solution)/shard_map/ppermute | solution.py:276
  29.6 7.9 %collective-permute-start.8 = (f32[2,64,512]{2,1,0:T(8,128)S(1)}, f32[2,64,512]{2,1,0:T(8,128)S(1)}, u32[]{:S(2)}, u32[]{:S(2)}) collective-permute-start(f32[2,64,512]{2,1,0:T(8,128)S(1)} %pad_maximum_fusion.3), channel_id=1, source_target_pairs={{0,2},{32,34},{64,66},{96,98},{128,130},{160,162},{192,194},{224,2... | collective-permute-start | bytes 786440 | tf_op jit(solution)/shard_map/ppermute | solution.py:276
  34.1 23.2 %collective-permute-start.10 = (f32[256,512]{1,0:T(8,128)}, f32[256,512]{1,0:T(8,128)}, u32[]{:S(2)}, u32[]{:S(2)}) collective-permute-start(f32[256,512]{1,0:T(8,128)} %get-tuple-element.55), channel_id=1, source_target_pairs={{0,4},{1,5},{32,36},{33,37},{64,68},{65,69},{96,100},{97,101},{128... | collective-permute-start | bytes 1572872 | tf_op jit(solution)/shard_map/ppermute | solution.py:276
  35.3 23.3 %collective-permute-start.11 = (f32[256,512]{1,0:T(8,128)}, f32[256,512]{1,0:T(8,128)}, u32[]{:S(2)}, u32[]{:S(2)}) collective-permute-start(f32[256,512]{1,0:T(8,128)} %get-tuple-element.54), channel_id=1, source_target_pairs={{0,8},{1,9},{32,40},{33,41},{64,72},{65,73},{96,104},{97,105},{128... | collective-permute-start | bytes 1572872 | tf_op jit(solution)/shard_map/ppermute | solution.py:276
  37.5 24.0 %collective-permute-start.9 = (f32[2,64,512]{2,1,0:T(8,128)S(1)}, f32[2,64,512]{2,1,0:T(8,128)S(1)}, u32[]{:S(2)}, u32[]{:S(2)}) collective-permute-start(f32[2,64,512]{2,1,0:T(8,128)S(1)} %broadcast_select_fusion.5), channel_id=1, source_target_pairs={{0,1},{2,3},{32,33},{34,35},{64,65},{66,67},{96,97},{98,99},{128,1... | collective-permute-start | bytes 786440 | tf_op jit(solution)/shard_map/ppermute | solution.py:276
  38.3 21.8 %collective-permute-start.6 = (f32[1,64,512]{2,1,0:T(8,128)S(1)}, f32[1,64,512]{2,1,0:T(8,128)S(1)}, u32[]{:S(2)}, u32[]{:S(2)}) collective-permute-start(f32[1,64,512]{2,1,0:T(8,128)S(1)} %broadcast_select_fusion.10), channel_id=1, source_target_pairs={{0,16},{1,17},{2,18},{3,19},{32,48},{33,49},{34,50},{35,51},{64,80... | collective-permute-start | bytes 393224 | tf_op jit(solution)/shard_map/ppermute | solution.py:276
  38.9 24.9 %collective-permute-start.12 = (f32[256,512]{1,0:T(8,128)S(1)}, f32[256,512]{1,0:T(8,128)}, u32[]{:S(2)}, u32[]{:S(2)}) collective-permute-start(f32[256,512]{1,0:T(8,128)S(1)} %get-tuple-element.53), channel_id=1, source_target_pairs={{0,12},{1,13},{32,44},{33,45},{64,76},{65,77},{96,108},{97,109},{1... | collective-permute-start | bytes 1572872 | tf_op jit(solution)/shard_map/ppermute | solution.py:276
  57.2 6.6 %collective-permute-start.13 = (f32[256,512]{1,0:T(8,128)S(1)}, f32[256,512]{1,0:T(8,128)}, u32[]{:S(2)}, u32[]{:S(2)}) collective-permute-start(f32[256,512]{1,0:T(8,128)S(1)} %get-tuple-element.52), channel_id=1, source_target_pairs={{0,16},{1,17},{32,48},{33,49},{64,80},{65,81},{96,112},{97,113},{1... | collective-permute-start | bytes 1572872 | tf_op jit(solution)/shard_map/ppermute | solution.py:276
  58.7 5.2 %collective-permute-start.14 = (f32[256,512]{1,0:T(8,128)S(1)}, f32[256,512]{1,0:T(8,128)}, u32[]{:S(2)}, u32[]{:S(2)}) collective-permute-start(f32[256,512]{1,0:T(8,128)S(1)} %get-tuple-element.51), channel_id=1, source_target_pairs={{0,20},{1,21},{32,52},{33,53},{64,84},{65,85},{96,116},{97,117},{1... | collective-permute-start | bytes 1572872 | tf_op jit(solution)/shard_map/ppermute | solution.py:276
  65.7 5.4 %collective-permute-start.17 = (f32[64,512]{1,0:T(8,128)S(1)}, f32[64,512]{1,0:T(8,128)S(1)}, u32[]{:S(2)}, u32[]{:S(2)}) collective-permute-start(f32[64,512]{1,0:T(8,128)S(1)} %get-tuple-element.61), channel_id=1, source_target_pairs={{0,1},{1,2},{4,5},{5,6},{8,9},{9,10},{12,13},{13,14},{16,17},{17,1... | collective-permute-start | bytes 393224 | tf_op jit(solution)/shard_map/ppermute | solution.py:276
  69.1 5.7 %collective-permute-start.19 = (f32[64,512]{1,0:T(8,128)S(1)}, f32[64,512]{1,0:T(8,128)S(1)}, u32[]{:S(2)}, u32[]{:S(2)}) collective-permute-start(f32[64,512]{1,0:T(8,128)S(1)} %get-tuple-element.62), channel_id=1, source_target_pairs={{0,3},{1,0},{4,7},{5,4},{8,11},{9,8},{12,15},{13,12},{16,19},{17,1... | collective-permute-start | bytes 393224 | tf_op jit(solution)/shard_map/ppermute | solution.py:276
  77.2 43.4 %collective-permute-start.21 = (f32[1,64,512]{2,1,0:T(8,128)S(1)}, f32[1,64,512]{2,1,0:T(8,128)S(1)}, u32[]{:S(2)}, u32[]{:S(2)}) collective-permute-start(f32[1,64,512]{2,1,0:T(8,128)S(1)} %broadcast_select_fusion.7), channel_id=1, source_target_pairs={{0,4},{1,5},{2,6},{3,7},{8,12},{9,13},{10,14},{11,15},{16,20},{17,... | collective-permute-start | bytes 393224 | tf_op jit(solution)/shard_map/ppermute | solution.py:276
  78.6 43.6 %collective-permute-start.27 = (f32[2,64,512]{2,1,0:T(8,128)S(1)}, f32[2,64,512]{2,1,0:T(8,128)S(1)}, u32[]{:S(2)}, u32[]{:S(2)}) collective-permute-start(f32[2,64,512]{2,1,0:T(8,128)S(1)} %broadcast_select_fusion.2), channel_id=1, source_target_pairs={{0,8},{1,9},{2,10},{3,11},{16,24},{17,25},{18,26},{19,27},{32,40},... | collective-permute-start | bytes 786440 | tf_op jit(solution)/shard_map/ppermute | solution.py:276
  120.7 5.5 %collective-permute-start.23 = (f32[1,64,512]{2,1,0:T(8,128)S(1)}, f32[1,64,512]{2,1,0:T(8,128)S(1)}, u32[]{:S(2)}, u32[]{:S(2)}) collective-permute-start(f32[1,64,512]{2,1,0:T(8,128)S(1)} %broadcast_select_fusion.8), channel_id=1, source_target_pairs={{0,128},{1,129},{2,130},{3,131},{4,132},{5,133},{6,134},{7,135},{8... | collective-permute-start | bytes 393224 | tf_op jit(solution)/shard_map/ppermute | solution.py:276
  121.1 6.5 %collective-permute-start.24 = (f32[1,64,512]{2,1,0:T(8,128)S(1)}, f32[1,64,512]{2,1,0:T(8,128)S(1)}, u32[]{:S(2)}, u32[]{:S(2)}) collective-permute-start(f32[1,64,512]{2,1,0:T(8,128)S(1)} %broadcast_select_fusion.8), channel_id=1, source_target_pairs={{0,192},{1,193},{2,194},{3,195},{4,196},{5,197},{6,198},{7,199},{8... | collective-permute-start | bytes 393224 | tf_op jit(solution)/shard_map/ppermute | solution.py:276
  122.2 20.6 %collective-permute-start.28 = (f32[2,64,512]{2,1,0:T(8,128)S(1)}, f32[2,64,512]{2,1,0:T(8,128)S(1)}, u32[]{:S(2)}, u32[]{:S(2)}) collective-permute-start(f32[2,64,512]{2,1,0:T(8,128)S(1)} %broadcast_select_fusion.3), channel_id=1, source_target_pairs={{0,4},{1,5},{2,6},{3,7},{8,12},{9,13},{10,14},{11,15},{16,20},{17,... | collective-permute-start | bytes 786440 | tf_op jit(solution)/shard_map/ppermute | solution.py:276
  127.6 31.3 %collective-permute-start.25 = (f32[4,1,64,512]{3,2,1,0:T(8,128)S(1)}, f32[4,1,64,512]{3,2,1,0:T(8,128)}, u32[]{:S(2)}, u32[]{:S(2)}) collective-permute-start(f32[4,1,64,512]{3,2,1,0:T(8,128)S(1)} %pad_maximum_fusion.1.mine_ref), channel_id=1, source_target_pairs={{0,32},{1,33},{2,34},{3,35},{4,36},{5,37},{6,38},{7,39},{8,40},{9,... | collective-permute-start | bytes 1572872 | tf_op jit(solution)/shard_map/ppermute | solution.py:276
  139.3 18.0 %collective-permute-start.29 = (f32[2,64,512]{2,1,0:T(8,128)S(1)}, f32[2,64,512]{2,1,0:T(8,128)S(1)}, u32[]{:S(2)}, u32[]{:S(2)}) collective-permute-start(f32[2,64,512]{2,1,0:T(8,128)S(1)} %copy-done.1), channel_id=1, source_target_pairs={{0,0},{1,32},{2,64},{3,96},{4,128},{5,160},{6,192},{7,224},{32,1},... | collective-permute-start | bytes 786440 | tf_op jit(solution)/shard_map/ppermute | solution.py:276
  157.4 23.3 %collective-permute-start.30 = (f32[4,64,512]{2,1,0:T(8,128)S(1)}, f32[4,64,512]{2,1,0:T(8,128)S(1)}, u32[]{:S(2)}, u32[]{:S(2)}) collective-permute-start(f32[4,64,512]{2,1,0:T(8,128)S(1)} %pad_maximum_fusion.2), channel_id=1, source_target_pairs={{0,64},{1,65},{2,66},{3,67},{4,68},{5,69},{6,70},{7,71},{8,72},{9,... | collective-permute-start | bytes 1572872 | tf_op jit(solution)/shard_map/ppermute | solution.py:276
  157.5 23.2 %collective-permute-start.31 = (f32[4,64,512]{2,1,0:T(8,128)S(1)}, f32[4,64,512]{2,1,0:T(8,128)S(1)}, u32[]{:S(2)}, u32[]{:S(2)}) collective-permute-start(f32[4,64,512]{2,1,0:T(8,128)S(1)} %pad_maximum_fusion.2), channel_id=1, source_target_pairs={{0,128},{1,129},{2,130},{3,131},{4,132},{5,133},{6,134},{7,135},{8... | collective-permute-start | bytes 1572872 | tf_op jit(solution)/shard_map/ppermute | solution.py:276
  157.6 26.8 %collective-permute-start.32 = (f32[4,64,512]{2,1,0:T(8,128)S(1)}, f32[4,64,512]{2,1,0:T(8,128)S(1)}, u32[]{:S(2)}, u32[]{:S(2)}) collective-permute-start(f32[4,64,512]{2,1,0:T(8,128)S(1)} %pad_maximum_fusion.2), channel_id=1, source_target_pairs={{0,192},{1,193},{2,194},{3,195},{4,196},{5,197},{6,198},{7,199},{8... | collective-permute-start | bytes 1572872 | tf_op jit(solution)/shard_map/ppermute | solution.py:276
  (17 other events, 131.3 us)
Sparse Core Ops, SparseCore 0:
  75.8 134.3 all-gather.2
where the time goes:
time: 259 us; the launch traced here: 258 us
  waiting for transfers between devices  102 us (39%)
  Pallas kernels  81.5 us (31%)
  starting transfers between devices  45.4 us (18%)
  between operations  14 us (5%)
  other arithmetic  7.99 us (3%)
  local copies, waits for them, and re-layouts  6.54 us (3%)
    ppermute x34, waiting for transfers between devices, permute(): return lax.ppermute(v, AX, [(lin(*a), lin(*b)) for a, b in pairs])  102 us
    ppermute x34, starting transfers between devices, permute(): return lax.ppermute(v, AX, [(lin(*a), lin(*b)) for a, b in pairs])  45.4 us
    pallas_call x1, Pallas kernels, factor_second(): pl.pallas_call(second_kernel, out_shape=square(3), in_specs=[SMEM, VMEM,...  27 us
    pallas_call x1, Pallas kernels, finish(): pl.pallas_call(finish_kernel, out_shape=jax.ShapeDtypeStruct(local.shape,...  26 us
    pallas_call x1, Pallas kernels, factor_first(): pl.pallas_call(first_kernel, out_shape=square(2), in_specs=[SMEM, VMEM, V...  21.7 us
    pallas_call x1, Pallas kernels, prepare(): pl.pallas_call(prepare_kernel, out_shape=square(2), in_specs=[SMEM] + [VM...  6.79 us
  transfers between devices with their start and end apart: 35, of which 13 were waited for; matrix products, arithmetic and copies ran while one was open for 3% of the time, Pallas kernels for 22%

commit v1 on v0

--- a/solution.py
+++ b/solution.py
@@ -356,7 +356,8 @@
     beside = permute(mine[1], [((r, 1), (r, 0)) for r in range(ROWS)])
     second = spread_x(jnp.stack([mine[1], beside]), x)
     first, second, arrived = lax.optimization_barrier((first, second, arrived))
-    first, second = spread_z(first, z, (2, 1)), spread_z(second, z, (4, 2, 1))
+    first = spread_z(first, z, (2,))
+    first, second = spread_z(first, z, (1,)), spread_z(second, z, (4, 2, 1))
     first = with_partner(ring(first))
 
     dealt = pick([(z == 0, eighth(0))] + [(z == k, arrived[k - 1]) for k in range(1, 8)])
@@ -370,10 +371,10 @@
     panels = lax.all_gather(piece, "col")
 
     pairs = [((r, 8 * s + q), (q, 8 * s + r)) for s in range(slots) for r in range(ROWS) for q in range(ROWS)]
-    rest = ring(jnp.concatenate([second, permute(piece, pairs)]))
+    crossed = permute(piece, pairs)
     factor0, inverse0 = factor_first(where, *first)
-    inverse0, rest = lax.optimization_barrier((inverse0, rest))
-    rest = with_partner(rest)
+    inverse0, second, crossed = lax.optimization_barrier((inverse0, second, crossed))
+    rest = with_partner(ring(jnp.concatenate([second, crossed])))
     p01, factor1, inverse1 = factor_second(where, *rest, inverse0)
     p0j, p1j = prepare(where, *rest, inverse0, p01, inverse1)
 

time: 259 us -> 274 us (1.058)
  waiting for transfers between devices: 102 us -> 119 us
    ppermute x34, waiting for transfers between devices: 102 us -> 119 us  [permute(): return lax.ppermute(v, AX, [(lin(*a), lin(*b)) for a, b in pairs])]
  transfers between devices with their start and end apart: 35 -> 35, of which waited for: 13 -> 15; matrix products, arithmetic and copies ran while one was open for 3% -> 2% of each run, Pallas kernels for 22% -> 20%
where the time goes in v1:
time: 274 us; the launch traced here: 273 us
  waiting for transfers between devices  119 us (43%)
  Pallas kernels  81.3 us (30%)
  starting transfers between devices  45.6 us (17%)
  between operations  14 us (5%)
  local copies, waits for them, and re-layouts  6.59 us (2%)
  other arithmetic  6.47 us (2%)
    ppermute x34, waiting for transfers between devices, permute(): return lax.ppermute(v, AX, [(lin(*a), lin(*b)) for a, b in pairs])  119 us
    ppermute x34, starting transfers between devices, permute(): return lax.ppermute(v, AX, [(lin(*a), lin(*b)) for a, b in pairs])  45.6 us
    pallas_call x1, Pallas kernels, factor_second(): pl.pallas_call(second_kernel, out_shape=square(3), in_specs=[SMEM, VMEM,...  26.8 us
    pallas_call x1, Pallas kernels, finish(): pl.pallas_call(finish_kernel, out_shape=jax.ShapeDtypeStruct(local.shape,...  26 us
    pallas_call x1, Pallas kernels, factor_first(): pl.pallas_call(first_kernel, out_shape=square(2), in_specs=[SMEM, VMEM, V...  21.7 us
    pallas_call x1, Pallas kernels, prepare(): pl.pallas_call(prepare_kernel, out_shape=square(2), in_specs=[SMEM] + [VM...  6.8 us
  transfers between devices with their start and end apart: 35, of which 15 were waited for; matrix products, arithmetic and copies ran while one was open for 2% of the time, Pallas kernels for 20%

profile of v1, /device:TPU:57, one launch (start us, length us, event | category | flops | bytes accessed | tf_op | source)
XLA Modules:
  0.0 273.1 jit_solution(15351354017985852740)
XLA Ops:
  8.6 2.3 collective-permute-done
  12.6 2.2 collective-permute-start.2
  14.8 5.2 %collective-permute-done.1 = f32[2,64,512]{2,1,0:T(8,128)S(1)} collective-permute-done((f32[2,64,512]{2,1,0:T(8,128)S(1)}, f32[2,64,512]{2,1,0:T(8,128)S(1)}, u32[]{:S(2)}, u32[]{:S(2)}) %collective-permute-start.1) | collective-permute-done | bytes 262176 | tf_op jit(solution)/shard_map/ppermute | solution.py:276
  21.6 6.4 %collective-permute-done.3 = f32[2,64,512]{2,1,0:T(8,128)S(1)} collective-permute-done((f32[2,64,512]{2,1,0:T(8,128)S(1)}, f32[2,64,512]{2,1,0:T(8,128)S(1)}, u32[]{:S(2)}, u32[]{:S(2)}) %collective-permute-start.3) | collective-permute-done | bytes 262176 | tf_op jit(solution)/shard_map/ppermute | solution.py:276
  30.4 3.7 %dynamic-slice_bitcast_fusion = (f32[256,512]{1,0:T(8,128)S(1)}, f32[256,512]{1,0:T(8,128)S(1)}, f32[256,512]{1,0:T(8,128)S(1)}, f32[256,512]{1,0:T(8,128)S(1)},...) fusion(f32[8,256,512]{2,1,0:T(8,128)} %bitcast.73, s32[]{:T(128)S(6)} %select_n.432, ...), kind=kLoop, calls=%fused_computation.13 | loop fusion | bytes 7340060 | tf_op jit(solution)/shard_map/jit(dynamic_index_in_dim)/squeeze | solution.py:344
  40.4 16.8 %collective-permute-done.10 = f32[256,512]{1,0:T(8,128)} collective-permute-done((f32[256,512]{1,0:T(8,128)}, f32[256,512]{1,0:T(8,128)}, u32[]{:S(2)}, u32[]{:S(2)}) %collective-permute-start.10) | collective-permute-done | bytes 524320 | tf_op jit(solution)/shard_map/ppermute | solution.py:276
  63.9 1.8 fusion.6
  65.7 2.1 collective-permute-start.17
  69.1 1.9 collective-permute-start.19
  71.1 3.7 %collective-permute-done.19 = f32[64,512]{1,0:T(8,128)S(1)} collective-permute-done((f32[64,512]{1,0:T(8,128)S(1)}, f32[64,512]{1,0:T(8,128)S(1)}, u32[]{:S(2)}, u32[]{:S(2)}) %collective-permute-start.19) | collective-permute-done | bytes 131104 | tf_op jit(solution)/shard_map/ppermute | solution.py:276
  79.3 41.4 %collective-permute-done.21 = f32[1,64,512]{2,1,0:T(8,128)S(1)} collective-permute-done((f32[1,64,512]{2,1,0:T(8,128)S(1)}, f32[1,64,512]{2,1,0:T(8,128)S(1)}, u32[]{:S(2)}, u32[]{:S(2)}) %collective-permute-start.21) | collective-permute-done | bytes 131104 | tf_op jit(solution)/shard_map/ppermute | solution.py:276
  122.2 2.3 collective-permute-done.22
  124.5 1.7 collective-permute-done.23
  127.6 10.5 %collective-permute-start.25 = (f32[4,1,64,512]{3,2,1,0:T(8,128)S(1)}, f32[4,1,64,512]{3,2,1,0:T(8,128)S(1)}, u32[]{:S(2)}, u32[]{:S(2)}) collective-permute-start(f32[4,1,64,512]{3,2,1,0:T(8,128)S(1)} %pad_maximum_fusion.1.mine_ref), channel_id=1, source_target_pairs={{0,32},{1,33},{2,34},{3,35},{4,36},{5,37},{6,38},{7,39},{8,40},{9,... | collective-permute-start | bytes 1572872 | tf_op jit(solution)/shard_map/ppermute | solution.py:276
  140.1 3.8 %collective-permute-start.29 = (f32[2,64,512]{2,1,0:T(8,128)S(1)}, f32[2,64,512]{2,1,0:T(8,128)S(1)}, u32[]{:S(2)}, u32[]{:S(2)}) collective-permute-start(f32[2,64,512]{2,1,0:T(8,128)S(1)} %copy-done.1), channel_id=1, source_target_pairs={{0,0},{1,32},{2,64},{3,96},{4,128},{5,160},{6,192},{7,224},{32,1},... | collective-permute-start | bytes 786440 | tf_op jit(solution)/shard_map/ppermute | solution.py:276
  143.8 7.6 %collective-permute-done.28 = f32[2,64,512]{2,1,0:T(8,128)S(1)} collective-permute-done((f32[2,64,512]{2,1,0:T(8,128)S(1)}, f32[2,64,512]{2,1,0:T(8,128)S(1)}, u32[]{:S(2)}, u32[]{:S(2)}) %collective-permute-start.28) | collective-permute-done | bytes 262176 | tf_op jit(solution)/shard_map/ppermute | solution.py:276
  152.3 21.7 %factor_first.1 = (f32[512,512]{1,0:T(8,128)}, f32[512,512]{1,0:T(8,128)}) custom-call(s32[2]{0:T(128)} %pad_add_fusion.where_ref, f32[4,1,64,512]{3,2,1,0:T(8,128)} %copy-done.2, f32[4,1,64,512]{3,2,1,0:T(8,128)} %copy-done.4), custom_call_target="tpu_custom_call" | custom-call | flops 10000000000 | bytes 3145728 | tf_op jit(solution)/shard_map/factor_first/pallas_call | solution.py:116
  175.8 11.0 %collective-permute-done.30 = f32[4,64,512]{2,1,0:T(8,128)S(1)} collective-permute-done((f32[4,64,512]{2,1,0:T(8,128)S(1)}, f32[4,64,512]{2,1,0:T(8,128)S(1)}, u32[]{:S(2)}, u32[]{:S(2)}) %collective-permute-start.30) | collective-permute-done | bytes 524320 | tf_op jit(solution)/shard_map/ppermute | solution.py:276
  186.7 2.2 collective-permute-done.31
  189.0 12.7 %collective-permute-done.32 = f32[4,64,512]{2,1,0:T(8,128)S(1)} collective-permute-done((f32[4,64,512]{2,1,0:T(8,128)S(1)}, f32[4,64,512]{2,1,0:T(8,128)S(1)}, u32[]{:S(2)}, u32[]{:S(2)}) %collective-permute-start.32) | collective-permute-done | bytes 524320 | tf_op jit(solution)/shard_map/ppermute | solution.py:276
  203.8 2.8 %collective-permute-done.33.other_ref = f32[4,4,64,512]{3,2,1,0:T(8,128)} collective-permute-done((f32[4,4,64,512]{3,2,1,0:T(8,128)S(1)}, f32[4,4,64,512]{3,2,1,0:T(8,128)}, u32[]{:S(2)}, u32[]{:S(2)}) %collective-permute-start.33) | collective-permute-done | bytes 2097184 | tf_op jit(solution)/shard_map/ppermute | solution.py:276
  206.6 26.8 %factor_second.1 = (f32[512,512]{1,0:T(8,128)}, f32[512,512]{1,0:T(8,128)}, f32[512,512]{1,0:T(8,128)}) custom-call(s32[2]{0:T(128)} %pad_add_fusion.where_ref, f32[4,4,64,512]{3,2,1,0:T(8,128)} %copy-done, f32[4,4,64,512]{3,2,1,0:T(8,128)} %collective-permute-done.33.other_ref, f32[512,512]{1,0:T(8,128)} %get-tuple-element.34.v0_ref.v0), custom_call_target="tpu_custom_call" | custom-call | flops 10000000000 | bytes 6291456 | tf_op jit(solution)/shard_map/factor_second/pallas_call | solution.py:136
  233.5 6.8 %prepare.1 = (f32[512,512]{1,0:T(8,128)}, f32[512,512]{1,0:T(8,128)}) custom-call(s32[2]{0:T(128)} %pad_add_fusion.where_ref, f32[4,4,64,512]{3,2,1,0:T(8,128)} %copy-done, f32[4,4,64,512]{3,2,1,0:T(8,128)} %collective-permute-done.33.other_ref, f32[512,512]{1,0:T(8,128)} %get-tuple-element.34.v0_ref.v0, f32[512,512]{1,0:T(8,128)} %get-tuple-element.37.p01_ref.p01, ...), custom_call_target="tpu_custom_call" | custom-call | flops 3000000000 | bytes 9437184 | tf_op jit(solution)/shard_map/prepare/pallas_call | solution.py:169
  240.3 26.0 %finish.1 = f32[4,512,512]{2,1,0:T(8,128)} custom-call(s32[4]{0:T(128)} %and_select_fusion.at_ref, s32[4]{0:T(128)} %broadcast_select_fusion.13.kind_ref, f32[32,2,64,512]{3,2,1,0:T(8,128)} %bitcast.89, f32[4,512,512]{2,1,0:T(8,128)} %bitcast.75, f32[512,512]{1,0:T(8,128)} %get-tuple-element.34.v0_ref.v0, f32[512,512]{1,0:T(8,128)} %get-tuple-element.37.p01_ref.p01, ...), custom_call_target="tpu_custom_call" | custom-call | flops 30000001024 | bytes 25165824 | tf_op jit(solution)/shard_map/finish/pallas_call | solution.py:244
  (90 shorter events, 35.6 us)
Async XLA Ops:
  6.5 233.7 %all-gather.3.cloned.1.call-start = ((), (), s32[]{:S(2)}) async-start(), calls=%async_computation | async-start | bytes 8650752 | tf_op jit(solution)/shard_map/all_gather | solution.py:371
  12.5 7.6 %collective-permute-start.1 = (f32[2,64,512]{2,1,0:T(8,128)S(1)}, f32[2,64,512]{2,1,0:T(8,128)S(1)}, u32[]{:S(2)}, u32[]{:S(2)}) collective-permute-start(f32[2,64,512]{2,1,0:T(8,128)S(1)} %get-tuple-element.52), channel_id=1, source_target_pairs={{0,64},{1,65},{2,66},{3,67},{4,68},{5,69},{6,70},{7,71},{8,72},{9,... | collective-permute-start | bytes 786440 | tf_op jit(solution)/shard_map/ppermute | solution.py:276
  12.6 9.0 %collective-permute-start.2 = (f32[2,64,512]{2,1,0:T(8,128)S(1)}, f32[2,64,512]{2,1,0:T(8,128)S(1)}, u32[]{:S(2)}, u32[]{:S(2)}) collective-permute-start(f32[2,64,512]{2,1,0:T(8,128)S(1)} %get-tuple-element.53), channel_id=1, source_target_pairs={{0,128},{1,129},{2,130},{3,131},{4,132},{5,133},{6,134},{7,135},{8... | collective-permute-start | bytes 786440 | tf_op jit(solution)/shard_map/ppermute | solution.py:276
  14.8 13.2 %collective-permute-start.3 = (f32[2,64,512]{2,1,0:T(8,128)S(1)}, f32[2,64,512]{2,1,0:T(8,128)S(1)}, u32[]{:S(2)}, u32[]{:S(2)}) collective-permute-start(f32[2,64,512]{2,1,0:T(8,128)S(1)} %get-tuple-element.54), channel_id=1, source_target_pairs={{0,192},{1,193},{2,194},{3,195},{4,196},{5,197},{6,198},{7,199},{8... | collective-permute-start | bytes 786440 | tf_op jit(solution)/shard_map/ppermute | solution.py:276
  29.6 7.9 %collective-permute-start.8 = (f32[2,64,512]{2,1,0:T(8,128)S(1)}, f32[2,64,512]{2,1,0:T(8,128)S(1)}, u32[]{:S(2)}, u32[]{:S(2)}) collective-permute-start(f32[2,64,512]{2,1,0:T(8,128)S(1)} %pad_maximum_fusion.2), channel_id=1, source_target_pairs={{0,2},{32,34},{64,66},{96,98},{128,130},{160,162},{192,194},{224,2... | collective-permute-start | bytes 786440 | tf_op jit(solution)/shard_map/ppermute | solution.py:276
  34.1 23.2 %collective-permute-start.10 = (f32[256,512]{1,0:T(8,128)}, f32[256,512]{1,0:T(8,128)}, u32[]{:S(2)}, u32[]{:S(2)}) collective-permute-start(f32[256,512]{1,0:T(8,128)} %get-tuple-element.51), channel_id=1, source_target_pairs={{0,4},{1,5},{32,36},{33,37},{64,68},{65,69},{96,100},{97,101},{128... | collective-permute-start | bytes 1572872 | tf_op jit(solution)/shard_map/ppermute | solution.py:276
  35.3 23.3 %collective-permute-start.11 = (f32[256,512]{1,0:T(8,128)}, f32[256,512]{1,0:T(8,128)}, u32[]{:S(2)}, u32[]{:S(2)}) collective-permute-start(f32[256,512]{1,0:T(8,128)} %get-tuple-element.50), channel_id=1, source_target_pairs={{0,8},{1,9},{32,40},{33,41},{64,72},{65,73},{96,104},{97,105},{128... | collective-permute-start | bytes 1572872 | tf_op jit(solution)/shard_map/ppermute | solution.py:276
  37.6 24.0 %collective-permute-start.9 = (f32[2,64,512]{2,1,0:T(8,128)S(1)}, f32[2,64,512]{2,1,0:T(8,128)S(1)}, u32[]{:S(2)}, u32[]{:S(2)}) collective-permute-start(f32[2,64,512]{2,1,0:T(8,128)S(1)} %broadcast_select_fusion.5), channel_id=1, source_target_pairs={{0,1},{2,3},{32,33},{34,35},{64,65},{66,67},{96,97},{98,99},{128,1... | collective-permute-start | bytes 786440 | tf_op jit(solution)/shard_map/ppermute | solution.py:276
  38.3 21.8 %collective-permute-start.6 = (f32[1,64,512]{2,1,0:T(8,128)S(1)}, f32[1,64,512]{2,1,0:T(8,128)S(1)}, u32[]{:S(2)}, u32[]{:S(2)}) collective-permute-start(f32[1,64,512]{2,1,0:T(8,128)S(1)} %broadcast_select_fusion.10), channel_id=1, source_target_pairs={{0,16},{1,17},{2,18},{3,19},{32,48},{33,49},{34,50},{35,51},{64,80... | collective-permute-start | bytes 393224 | tf_op jit(solution)/shard_map/ppermute | solution.py:276
  39.0 24.9 %collective-permute-start.12 = (f32[256,512]{1,0:T(8,128)S(1)}, f32[256,512]{1,0:T(8,128)}, u32[]{:S(2)}, u32[]{:S(2)}) collective-permute-start(f32[256,512]{1,0:T(8,128)S(1)} %get-tuple-element.49), channel_id=1, source_target_pairs={{0,12},{1,13},{32,44},{33,45},{64,76},{65,77},{96,108},{97,109},{1... | collective-permute-start | bytes 1572872 | tf_op jit(solution)/shard_map/ppermute | solution.py:276
  57.2 6.7 %collective-permute-start.13 = (f32[256,512]{1,0:T(8,128)S(1)}, f32[256,512]{1,0:T(8,128)}, u32[]{:S(2)}, u32[]{:S(2)}) collective-permute-start(f32[256,512]{1,0:T(8,128)S(1)} %get-tuple-element.48), channel_id=1, source_target_pairs={{0,16},{1,17},{32,48},{33,49},{64,80},{65,81},{96,112},{97,113},{1... | collective-permute-start | bytes 1572872 | tf_op jit(solution)/shard_map/ppermute | solution.py:276
  58.7 5.2 %collective-permute-start.14 = (f32[256,512]{1,0:T(8,128)S(1)}, f32[256,512]{1,0:T(8,128)}, u32[]{:S(2)}, u32[]{:S(2)}) collective-permute-start(f32[256,512]{1,0:T(8,128)S(1)} %get-tuple-element.47), channel_id=1, source_target_pairs={{0,20},{1,21},{32,52},{33,53},{64,84},{65,85},{96,116},{97,117},{1... | collective-permute-start | bytes 1572872 | tf_op jit(solution)/shard_map/ppermute | solution.py:276
  65.7 5.4 %collective-permute-start.17 = (f32[64,512]{1,0:T(8,128)S(1)}, f32[64,512]{1,0:T(8,128)S(1)}, u32[]{:S(2)}, u32[]{:S(2)}) collective-permute-start(f32[64,512]{1,0:T(8,128)S(1)} %get-tuple-element.57), channel_id=1, source_target_pairs={{0,1},{1,2},{4,5},{5,6},{8,9},{9,10},{12,13},{13,14},{16,17},{17,1... | collective-permute-start | bytes 393224 | tf_op jit(solution)/shard_map/ppermute | solution.py:276
  69.1 5.7 %collective-permute-start.19 = (f32[64,512]{1,0:T(8,128)S(1)}, f32[64,512]{1,0:T(8,128)S(1)}, u32[]{:S(2)}, u32[]{:S(2)}) collective-permute-start(f32[64,512]{1,0:T(8,128)S(1)} %get-tuple-element.58), channel_id=1, source_target_pairs={{0,3},{1,0},{4,7},{5,4},{8,11},{9,8},{12,15},{13,12},{16,19},{17,1... | collective-permute-start | bytes 393224 | tf_op jit(solution)/shard_map/ppermute | solution.py:276
  77.2 43.4 %collective-permute-start.21 = (f32[1,64,512]{2,1,0:T(8,128)S(1)}, f32[1,64,512]{2,1,0:T(8,128)S(1)}, u32[]{:S(2)}, u32[]{:S(2)}) collective-permute-start(f32[1,64,512]{2,1,0:T(8,128)S(1)} %broadcast_select_fusion.7), channel_id=1, source_target_pairs={{0,4},{1,5},{2,6},{3,7},{8,12},{9,13},{10,14},{11,15},{16,20},{17,... | collective-permute-start | bytes 393224 | tf_op jit(solution)/shard_map/ppermute | solution.py:276
  78.6 59.6 %collective-permute-start.27 = (f32[2,64,512]{2,1,0:T(8,128)S(1)}, f32[2,64,512]{2,1,0:T(8,128)S(1)}, u32[]{:S(2)}, u32[]{:S(2)}) collective-permute-start(f32[2,64,512]{2,1,0:T(8,128)S(1)} %broadcast_select_fusion.2), channel_id=1, source_target_pairs={{0,8},{1,9},{2,10},{3,11},{16,24},{17,25},{18,26},{19,27},{32,40},... | collective-permute-start | bytes 786440 | tf_op jit(solution)/shard_map/ppermute | solution.py:276
  120.7 5.5 %collective-permute-start.23 = (f32[1,64,512]{2,1,0:T(8,128)S(1)}, f32[1,64,512]{2,1,0:T(8,128)S(1)}, u32[]{:S(2)}, u32[]{:S(2)}) collective-permute-start(f32[1,64,512]{2,1,0:T(8,128)S(1)} %broadcast_select_fusion.8), channel_id=1, source_target_pairs={{0,128},{1,129},{2,130},{3,131},{4,132},{5,133},{6,134},{7,135},{8... | collective-permute-start | bytes 393224 | tf_op jit(solution)/shard_map/ppermute | solution.py:276
  121.1 6.5 %collective-permute-start.24 = (f32[1,64,512]{2,1,0:T(8,128)S(1)}, f32[1,64,512]{2,1,0:T(8,128)S(1)}, u32[]{:S(2)}, u32[]{:S(2)}) collective-permute-start(f32[1,64,512]{2,1,0:T(8,128)S(1)} %broadcast_select_fusion.8), channel_id=1, source_target_pairs={{0,192},{1,193},{2,194},{3,195},{4,196},{5,197},{6,198},{7,199},{8... | collective-permute-start | bytes 393224 | tf_op jit(solution)/shard_map/ppermute | solution.py:276
  127.6 23.9 %collective-permute-start.25 = (f32[4,1,64,512]{3,2,1,0:T(8,128)S(1)}, f32[4,1,64,512]{3,2,1,0:T(8,128)S(1)}, u32[]{:S(2)}, u32[]{:S(2)}) collective-permute-start(f32[4,1,64,512]{3,2,1,0:T(8,128)S(1)} %pad_maximum_fusion.1.mine_ref), channel_id=1, source_target_pairs={{0,32},{1,33},{2,34},{3,35},{4,36},{5,37},{6,38},{7,39},{8,40},{9,... | collective-permute-start | bytes 1572872 | tf_op jit(solution)/shard_map/ppermute | solution.py:276
  138.2 13.2 %collective-permute-start.28 = (f32[2,64,512]{2,1,0:T(8,128)S(1)}, f32[2,64,512]{2,1,0:T(8,128)S(1)}, u32[]{:S(2)}, u32[]{:S(2)}) collective-permute-start(f32[2,64,512]{2,1,0:T(8,128)S(1)} %broadcast_select_fusion.3), channel_id=1, source_target_pairs={{0,4},{1,5},{2,6},{3,7},{8,12},{9,13},{10,14},{11,15},{16,20},{17,... | collective-permute-start | bytes 786440 | tf_op jit(solution)/shard_map/ppermute | solution.py:276
  140.1 34.0 %collective-permute-start.29 = (f32[2,64,512]{2,1,0:T(8,128)S(1)}, f32[2,64,512]{2,1,0:T(8,128)S(1)}, u32[]{:S(2)}, u32[]{:S(2)}) collective-permute-start(f32[2,64,512]{2,1,0:T(8,128)S(1)} %copy-done.1), channel_id=1, source_target_pairs={{0,0},{1,32},{2,64},{3,96},{4,128},{5,160},{6,192},{7,224},{32,1},... | collective-permute-start | bytes 786440 | tf_op jit(solution)/shard_map/ppermute | solution.py:276
  174.1 12.7 %collective-permute-start.30 = (f32[4,64,512]{2,1,0:T(8,128)S(1)}, f32[4,64,512]{2,1,0:T(8,128)S(1)}, u32[]{:S(2)}, u32[]{:S(2)}) collective-permute-start(f32[4,64,512]{2,1,0:T(8,128)S(1)} %constant_dynamic-update-slice_fusion), channel_id=1, source_target_pairs={{0,64},{1,65},{2,66},{3,67},{4,68},{5,69},{6,70},{7,71},{8,72},{9,... | collective-permute-start | bytes 1572872 | tf_op jit(solution)/shard_map/ppermute | solution.py:276
  175.1 13.9 %collective-permute-start.31 = (f32[4,64,512]{2,1,0:T(8,128)S(1)}, f32[4,64,512]{2,1,0:T(8,128)S(1)}, u32[]{:S(2)}, u32[]{:S(2)}) collective-permute-start(f32[4,64,512]{2,1,0:T(8,128)S(1)} %constant_dynamic-update-slice_fusion), channel_id=1, source_target_pairs={{0,128},{1,129},{2,130},{3,131},{4,132},{5,133},{6,134},{7,135},{8... | collective-permute-start | bytes 1572872 | tf_op jit(solution)/shard_map/ppermute | solution.py:276
  175.6 26.1 %collective-permute-start.32 = (f32[4,64,512]{2,1,0:T(8,128)S(1)}, f32[4,64,512]{2,1,0:T(8,128)S(1)}, u32[]{:S(2)}, u32[]{:S(2)}) collective-permute-start(f32[4,64,512]{2,1,0:T(8,128)S(1)} %constant_dynamic-update-slice_fusion), channel_id=1, source_target_pairs={{0,192},{1,193},{2,194},{3,195},{4,196},{5,197},{6,198},{7,199},{8... | collective-permute-start | bytes 1572872 | tf_op jit(solution)/shard_map/ppermute | solution.py:276
  (16 other events, 121.3 us)
Sparse Core Ops, SparseCore 0:
  75.8 132.7 all-gather.2

commit v2 on v0

--- a/solution.py
+++ b/solution.py
@@ -156,13 +156,22 @@
     return one(a[0], b[0]) + (one(a[0], b[1]) + one(a[1], b[0]))
 
 
-def prepare_kernel(where_ref, mine_ref, other_ref, v0_ref, p01_ref, v1_ref, p0_ref, p1_ref, w_ref):
+def product3(a, b):
+    def one(p, q):
+        return jnp.dot(p, q, preferred_element_type=F32)
+
+    return one(a[0], b[0]) + (one(a[0], b[1]) + one(a[1], b[0]))
+
+
+def prepare_kernel(where_ref, mine_ref, other_ref, v0_ref, p01_ref, v1_ref, t0_ref, t1_ref, w_ref):
     assemble(w_ref, mine_ref, other_ref, 2, where_ref)
-    p0 = times_t3(split(w_ref[...]), split(v0_ref[...]))
-    p0_ref[...] = p0
+    v0, p01, v1 = split(v0_ref[...]), split(p01_ref[...]), split(v1_ref[...])
+    p0 = times_t3(split(w_ref[...]), v0)
     assemble(w_ref, mine_ref, other_ref, 3, where_ref)
-    next1 = w_ref[...] - times_t3(split(p0), split(p01_ref[...]))
-    p1_ref[...] = times_t3(split(next1), split(v1_ref[...]))
+    p1 = times_t3(split(w_ref[...] - times_t3(split(p0), p01)), v1)
+    t1 = product3(split(p1), v1)
+    t1_ref[...] = t1
+    t0_ref[...] = product3(split(p0 - product3(split(t1), p01)), v0)
 
 
 def prepare(where, mine, other, inverse0, p01, inverse1):
@@ -203,13 +212,11 @@
 
     @pl.when(kind == UPDATE_BOTH)
     def _():
-        p0 = times(raw(0), 0)
-        p1 = times(raw(1) - times(p0, 1), 2)
-        o_ref[0] = a_ref[0] - times(p0, 3) - times(p1, 4)
+        o_ref[0] = a_ref[0] - times(raw(0), 3) - times(raw(1), 4)
 
     @pl.when(kind == UPDATE_SECOND)
     def _():
-        o_ref[0] = a_ref[0] - times(times(raw(1), 2), 4)
+        o_ref[0] = a_ref[0] - times(raw(1), 4)
 
     @pl.when(kind == PANEL0)
     def _():

time: 259 us -> 253 us (0.977)
  the two profiles are of different devices: /device:TPU:57 before, /device:TPU:2 now
where the time goes in v2:
time: 253 us; the launch traced here: 250 us
  Pallas kernels  77 us (30%)
  starting transfers between devices  76.8 us (30%)
  waiting for transfers between devices  66.6 us (26%)
  between operations  14 us (6%)
  other arithmetic  8.71 us (3%)
  local copies, waits for them, and re-layouts  6.69 us (3%)
    ppermute x34, starting transfers between devices, permute(): return lax.ppermute(v, AX, [(lin(*a), lin(*b)) for a, b in pairs])  76.8 us
    ppermute x34, waiting for transfers between devices, permute(): return lax.ppermute(v, AX, [(lin(*a), lin(*b)) for a, b in pairs])  66.6 us
    pallas_call x1, Pallas kernels, factor_second(): pl.pallas_call(second_kernel, out_shape=square(3), in_specs=[SMEM, VMEM,...  27.2 us
    pallas_call x1, Pallas kernels, factor_first(): pl.pallas_call(first_kernel, out_shape=square(2), in_specs=[SMEM, VMEM, V...  21.7 us
    pallas_call x1, Pallas kernels, finish(): pl.pallas_call(finish_kernel, out_shape=jax.ShapeDtypeStruct(local.shape,...  18.9 us
    pallas_call x1, Pallas kernels, prepare(): pl.pallas_call(prepare_kernel, out_shape=square(2), in_specs=[SMEM] + [VM...  9.23 us
  transfers between devices with their start and end apart: 35, of which 17 were waited for; matrix products, arithmetic and copies ran while one was open for 3% of the time, Pallas kernels for 23%

profile of v2, /device:TPU:2, one launch (start us, length us, event | category | flops | bytes accessed | tf_op | source)
XLA Modules:
  0.0 249.8 jit_solution(6550320279964190766)
XLA Ops:
  8.0 2.6 %collective-permute-done = f32[512,512]{1,0:T(8,128)S(1)} collective-permute-done((f32[512,512]{1,0:T(8,128)S(1)}, f32[512,512]{1,0:T(8,128)S(1)}, u32[]{:S(2)}, u32[]{:S(2)}) %collective-permute-start) | collective-permute-done | bytes 1048608 | tf_op jit(solution)/shard_map/ppermute | solution.py:283
  13.9 2.9 %collective-permute-start.2 = (f32[2,64,512]{2,1,0:T(8,128)S(1)}, f32[2,64,512]{2,1,0:T(8,128)S(1)}, u32[]{:S(2)}, u32[]{:S(2)}) collective-permute-start(f32[2,64,512]{2,1,0:T(8,128)S(1)} %get-tuple-element.57), channel_id=1, source_target_pairs={{0,128},{1,129},{2,130},{3,131},{4,132},{5,133},{6,134},{7,135},{8... | collective-permute-start | bytes 786440 | tf_op jit(solution)/shard_map/ppermute | solution.py:283
  18.1 3.8 %collective-permute-done.1 = f32[2,64,512]{2,1,0:T(8,128)S(1)} collective-permute-done((f32[2,64,512]{2,1,0:T(8,128)S(1)}, f32[2,64,512]{2,1,0:T(8,128)S(1)}, u32[]{:S(2)}, u32[]{:S(2)}) %collective-permute-start.1) | collective-permute-done | bytes 262176 | tf_op jit(solution)/shard_map/ppermute | solution.py:283
  21.9 6.8 %collective-permute-done.2 = f32[2,64,512]{2,1,0:T(8,128)S(1)} collective-permute-done((f32[2,64,512]{2,1,0:T(8,128)S(1)}, f32[2,64,512]{2,1,0:T(8,128)S(1)}, u32[]{:S(2)}, u32[]{:S(2)}) %collective-permute-start.2) | collective-permute-done | bytes 262176 | tf_op jit(solution)/shard_map/ppermute | solution.py:283
  29.6 9.2 %collective-permute-start.7 = (f32[64,512]{1,0:T(8,128)S(1)}, f32[64,512]{1,0:T(8,128)S(1)}, u32[]{:S(2)}, u32[]{:S(2)}) collective-permute-start(f32[64,512]{1,0:T(8,128)S(1)} %get-tuple-element.66), channel_id=1, source_target_pairs={{1,0},{33,32},{65,64},{97,96},{129,128},{161,160},{193,192},{225,2... | collective-permute-start | bytes 393224 | tf_op jit(solution)/shard_map/ppermute | solution.py:283
  42.1 3.7 %dynamic-slice_bitcast_fusion = (f32[256,512]{1,0:T(8,128)S(1)}, f32[256,512]{1,0:T(8,128)S(1)}, f32[256,512]{1,0:T(8,128)S(1)}, f32[256,512]{1,0:T(8,128)S(1)},...) fusion(f32[8,256,512]{2,1,0:T(8,128)} %bitcast.73, s32[]{:T(128)S(6)} %select_n.432, ...), kind=kLoop, calls=%fused_computation.14 | loop fusion | bytes 7340060 | tf_op jit(solution)/shard_map/jit(dynamic_index_in_dim)/squeeze | solution.py:351
  52.6 5.4 %collective-permute-done.5 = f32[1,64,512]{2,1,0:T(8,128)S(1)} collective-permute-done((f32[1,64,512]{2,1,0:T(8,128)S(1)}, f32[1,64,512]{2,1,0:T(8,128)S(1)}, u32[]{:S(2)}, u32[]{:S(2)}) %collective-permute-start.5) | collective-permute-done | bytes 131104 | tf_op jit(solution)/shard_map/ppermute | solution.py:283
  63.5 7.3 %collective-permute-done.11 = f32[256,512]{1,0:T(8,128)} collective-permute-done((f32[256,512]{1,0:T(8,128)}, f32[256,512]{1,0:T(8,128)}, u32[]{:S(2)}, u32[]{:S(2)}) %collective-permute-start.11) | collective-permute-done | bytes 524320 | tf_op jit(solution)/shard_map/ppermute | solution.py:283
  79.5 5.3 %collective-permute-done.12 = f32[256,512]{1,0:T(8,128)} collective-permute-done((f32[256,512]{1,0:T(8,128)S(1)}, f32[256,512]{1,0:T(8,128)}, u32[]{:S(2)}, u32[]{:S(2)}) %collective-permute-start.12) | collective-permute-done | bytes 524320 | tf_op jit(solution)/shard_map/ppermute | solution.py:283
  84.8 8.1 %collective-permute-done.13 = f32[256,512]{1,0:T(8,128)} collective-permute-done((f32[256,512]{1,0:T(8,128)S(1)}, f32[256,512]{1,0:T(8,128)}, u32[]{:S(2)}, u32[]{:S(2)}) %collective-permute-start.13) | collective-permute-done | bytes 524320 | tf_op jit(solution)/shard_map/ppermute | solution.py:283
  94.5 5.6 %collective-permute-done.16 = f32[256,512]{1,0:T(8,128)} collective-permute-done((f32[256,512]{1,0:T(8,128)S(1)}, f32[256,512]{1,0:T(8,128)}, u32[]{:S(2)}, u32[]{:S(2)}) %collective-permute-start.16) | collective-permute-done | bytes 524320 | tf_op jit(solution)/shard_map/ppermute | solution.py:283
  104.9 3.9 %collective-permute-start.19 = (f32[64,512]{1,0:T(8,128)S(1)}, f32[64,512]{1,0:T(8,128)S(1)}, u32[]{:S(2)}, u32[]{:S(2)}) collective-permute-start(f32[64,512]{1,0:T(8,128)S(1)} %get-tuple-element.62), channel_id=1, source_target_pairs={{0,3},{1,0},{4,7},{5,4},{8,11},{9,8},{12,15},{13,12},{16,19},{17,1... | collective-permute-start | bytes 393224 | tf_op jit(solution)/shard_map/ppermute | solution.py:283
  113.6 4.1 %collective-permute-start.26 = (f32[2,64,512]{2,1,0:T(8,128)S(1)}, f32[2,64,512]{2,1,0:T(8,128)S(1)}, u32[]{:S(2)}, u32[]{:S(2)}) collective-permute-start(f32[2,64,512]{2,1,0:T(8,128)S(1)} %broadcast_select_fusion.6), channel_id=1, source_target_pairs={{0,16},{1,17},{2,18},{3,19},{32,48},{33,49},{34,50},{35,51},{64,80... | collective-permute-start | bytes 786440 | tf_op jit(solution)/shard_map/ppermute | solution.py:283
  119.1 4.4 %collective-permute-done.26 = f32[2,64,512]{2,1,0:T(8,128)S(1)} collective-permute-done((f32[2,64,512]{2,1,0:T(8,128)S(1)}, f32[2,64,512]{2,1,0:T(8,128)S(1)}, u32[]{:S(2)}, u32[]{:S(2)}) %collective-permute-start.26) | collective-permute-done | bytes 262176 | tf_op jit(solution)/shard_map/ppermute | solution.py:283
  126.4 4.5 %collective-permute-start.23 = (f32[1,64,512]{2,1,0:T(8,128)S(1)}, f32[1,64,512]{2,1,0:T(8,128)S(1)}, u32[]{:S(2)}, u32[]{:S(2)}) collective-permute-start(f32[1,64,512]{2,1,0:T(8,128)S(1)} %broadcast_select_fusion.8), channel_id=1, source_target_pairs={{0,128},{1,129},{2,130},{3,131},{4,132},{5,133},{6,134},{7,135},{8... | collective-permute-start | bytes 393224 | tf_op jit(solution)/shard_map/ppermute | solution.py:283
  136.1 5.9 %collective-permute-start.29 = (f32[2,64,512]{2,1,0:T(8,128)S(1)}, f32[2,64,512]{2,1,0:T(8,128)S(1)}, u32[]{:S(2)}, u32[]{:S(2)}) collective-permute-start(f32[2,64,512]{2,1,0:T(8,128)S(1)} %copy-done.1), channel_id=1, source_target_pairs={{0,0},{1,32},{2,64},{3,96},{4,128},{5,160},{6,192},{7,224},{32,1},... | collective-permute-start | bytes 786440 | tf_op jit(solution)/shard_map/ppermute | solution.py:283
  142.7 4.0 %collective-permute-done.29 = f32[2,64,512]{2,1,0:T(8,128)S(1)} collective-permute-done((f32[2,64,512]{2,1,0:T(8,128)S(1)}, f32[2,64,512]{2,1,0:T(8,128)S(1)}, u32[]{:S(2)}, u32[]{:S(2)}) %collective-permute-start.29) | collective-permute-done | bytes 262176 | tf_op jit(solution)/shard_map/ppermute | solution.py:283
  146.8 8.6 %collective-permute-start.30 = (f32[4,64,512]{2,1,0:T(8,128)S(1)}, f32[4,64,512]{2,1,0:T(8,128)S(1)}, u32[]{:S(2)}, u32[]{:S(2)}) collective-permute-start(f32[4,64,512]{2,1,0:T(8,128)S(1)} %pad_maximum_fusion.2), channel_id=1, source_target_pairs={{0,64},{1,65},{2,66},{3,67},{4,68},{5,69},{6,70},{7,71},{8,72},{9,... | collective-permute-start | bytes 1572872 | tf_op jit(solution)/shard_map/ppermute | solution.py:283
  156.6 2.5 %collective-permute-start.32 = (f32[4,64,512]{2,1,0:T(8,128)S(1)}, f32[4,64,512]{2,1,0:T(8,128)S(1)}, u32[]{:S(2)}, u32[]{:S(2)}) collective-permute-start(f32[4,64,512]{2,1,0:T(8,128)S(1)} %pad_maximum_fusion.2), channel_id=1, source_target_pairs={{0,192},{1,193},{2,194},{3,195},{4,196},{5,197},{6,198},{7,199},{8... | collective-permute-start | bytes 1572872 | tf_op jit(solution)/shard_map/ppermute | solution.py:283
  159.1 21.7 %factor_first.1 = (f32[512,512]{1,0:T(8,128)}, f32[512,512]{1,0:T(8,128)}) custom-call(s32[2]{0:T(128)} %pad_add_fusion.where_ref, f32[4,1,64,512]{3,2,1,0:T(8,128)} %copy-done.2, f32[4,1,64,512]{3,2,1,0:T(8,128)} %collective-permute-done.25.other_ref), custom_call_target="tpu_custom_call" | custom-call | flops 10000000000 | bytes 3145728 | tf_op jit(solution)/shard_map/factor_first/pallas_call | solution.py:116
  184.7 2.9 %collective-permute-done.33.other_ref = f32[4,4,64,512]{3,2,1,0:T(8,128)} collective-permute-done((f32[4,4,64,512]{3,2,1,0:T(8,128)S(1)}, f32[4,4,64,512]{3,2,1,0:T(8,128)}, u32[]{:S(2)}, u32[]{:S(2)}) %collective-permute-start.33) | collective-permute-done | bytes 2097184 | tf_op jit(solution)/shard_map/ppermute | solution.py:283
  187.6 27.2 %factor_second.1 = (f32[512,512]{1,0:T(8,128)}, f32[512,512]{1,0:T(8,128)}, f32[512,512]{1,0:T(8,128)}) custom-call(s32[2]{0:T(128)} %pad_add_fusion.where_ref, f32[4,4,64,512]{3,2,1,0:T(8,128)} %copy-done, f32[4,4,64,512]{3,2,1,0:T(8,128)} %collective-permute-done.33.other_ref, f32[512,512]{1,0:T(8,128)} %get-tuple-element.36.v0_ref.v0), custom_call_target="tpu_custom_call" | custom-call | flops 10000000000 | bytes 6291456 | tf_op jit(solution)/shard_map/factor_second/pallas_call | solution.py:136
  214.8 9.2 %prepare.1 = (f32[512,512]{1,0:T(8,128)}, f32[512,512]{1,0:T(8,128)}) custom-call(s32[2]{0:T(128)} %pad_add_fusion.where_ref, f32[4,4,64,512]{3,2,1,0:T(8,128)} %copy-done, f32[4,4,64,512]{3,2,1,0:T(8,128)} %collective-permute-done.33.other_ref, f32[512,512]{1,0:T(8,128)} %get-tuple-element.36.v0_ref.v0, f32[512,512]{1,0:T(8,128)} %get-tuple-element.41.p01_ref.p01, ...), custom_call_target="tpu_custom_call" | custom-call | flops 3000000000 | bytes 9437184 | tf_op jit(solution)/shard_map/prepare/pallas_call | solution.py:178
  224.1 18.9 %finish.1 = f32[4,512,512]{2,1,0:T(8,128)} custom-call(s32[4]{0:T(128)} %and_select_fusion.at_ref, s32[4]{0:T(128)} %broadcast_select_fusion.13.kind_ref, f32[32,2,64,512]{3,2,1,0:T(8,128)} %bitcast.89, f32[4,512,512]{2,1,0:T(8,128)} %bitcast.75, f32[512,512]{1,0:T(8,128)} %get-tuple-element.36.v0_ref.v0, f32[512,512]{1,0:T(8,128)} %get-tuple-element.41.p01_ref.p01, ...), custom_call_target="tpu_custom_call" | custom-call | flops 30000001024 | bytes 25165824 | tf_op jit(solution)/shard_map/finish/pallas_call | solution.py:251
  (91 shorter events, 56.9 us)
Async XLA Ops:
  6.5 217.5 %all-gather.3.cloned.1.call-start = ((), (), s32[]{:S(2)}) async-start(), calls=%async_computation | async-start | bytes 8650752 | tf_op jit(solution)/shard_map/all_gather | solution.py:377
  12.2 9.7 %collective-permute-start.1 = (f32[2,64,512]{2,1,0:T(8,128)S(1)}, f32[2,64,512]{2,1,0:T(8,128)S(1)}, u32[]{:S(2)}, u32[]{:S(2)}) collective-permute-start(f32[2,64,512]{2,1,0:T(8,128)S(1)} %get-tuple-element.56), channel_id=1, source_target_pairs={{0,64},{1,65},{2,66},{3,67},{4,68},{5,69},{6,70},{7,71},{8,72},{9,... | collective-permute-start | bytes 786440 | tf_op jit(solution)/shard_map/ppermute | solution.py:283
  13.9 14.8 %collective-permute-start.2 = (f32[2,64,512]{2,1,0:T(8,128)S(1)}, f32[2,64,512]{2,1,0:T(8,128)S(1)}, u32[]{:S(2)}, u32[]{:S(2)}) collective-permute-start(f32[2,64,512]{2,1,0:T(8,128)S(1)} %get-tuple-element.57), channel_id=1, source_target_pairs={{0,128},{1,129},{2,130},{3,131},{4,132},{5,133},{6,134},{7,135},{8... | collective-permute-start | bytes 786440 | tf_op jit(solution)/shard_map/ppermute | solution.py:283
  16.8 11.9 %collective-permute-start.3 = (f32[2,64,512]{2,1,0:T(8,128)S(1)}, f32[2,64,512]{2,1,0:T(8,128)S(1)}, u32[]{:S(2)}, u32[]{:S(2)}) collective-permute-start(f32[2,64,512]{2,1,0:T(8,128)S(1)} %get-tuple-element.58), channel_id=1, source_target_pairs={{0,192},{1,193},{2,194},{3,195},{4,196},{5,197},{6,198},{7,199},{8... | collective-permute-start | bytes 786440 | tf_op jit(solution)/shard_map/ppermute | solution.py:283
  29.6 11.7 %collective-permute-start.7 = (f32[64,512]{1,0:T(8,128)S(1)}, f32[64,512]{1,0:T(8,128)S(1)}, u32[]{:S(2)}, u32[]{:S(2)}) collective-permute-start(f32[64,512]{1,0:T(8,128)S(1)} %get-tuple-element.66), channel_id=1, source_target_pairs={{1,0},{33,32},{65,64},{97,96},{129,128},{161,160},{193,192},{225,2... | collective-permute-start | bytes 393224 | tf_op jit(solution)/shard_map/ppermute | solution.py:283
  41.3 10.0 %collective-permute-start.8 = (f32[2,64,512]{2,1,0:T(8,128)S(1)}, f32[2,64,512]{2,1,0:T(8,128)S(1)}, u32[]{:S(2)}, u32[]{:S(2)}) collective-permute-start(f32[2,64,512]{2,1,0:T(8,128)S(1)} %pad_maximum_fusion.3), channel_id=1, source_target_pairs={{0,2},{32,34},{64,66},{96,98},{128,130},{160,162},{192,194},{224,2... | collective-permute-start | bytes 786440 | tf_op jit(solution)/shard_map/ppermute | solution.py:283
  45.7 15.7 %collective-permute-start.10 = (f32[256,512]{1,0:T(8,128)}, f32[256,512]{1,0:T(8,128)}, u32[]{:S(2)}, u32[]{:S(2)}) collective-permute-start(f32[256,512]{1,0:T(8,128)} %get-tuple-element.55), channel_id=1, source_target_pairs={{0,4},{1,5},{32,36},{33,37},{64,68},{65,69},{96,100},{97,101},{128... | collective-permute-start | bytes 1572872 | tf_op jit(solution)/shard_map/ppermute | solution.py:283
  47.8 23.0 %collective-permute-start.11 = (f32[256,512]{1,0:T(8,128)}, f32[256,512]{1,0:T(8,128)}, u32[]{:S(2)}, u32[]{:S(2)}) collective-permute-start(f32[256,512]{1,0:T(8,128)} %get-tuple-element.54), channel_id=1, source_target_pairs={{0,8},{1,9},{32,40},{33,41},{64,72},{65,73},{96,104},{97,105},{128... | collective-permute-start | bytes 1572872 | tf_op jit(solution)/shard_map/ppermute | solution.py:283
  51.3 24.4 %collective-permute-start.9 = (f32[2,64,512]{2,1,0:T(8,128)S(1)}, f32[2,64,512]{2,1,0:T(8,128)S(1)}, u32[]{:S(2)}, u32[]{:S(2)}) collective-permute-start(f32[2,64,512]{2,1,0:T(8,128)S(1)} %broadcast_select_fusion.5), channel_id=1, source_target_pairs={{0,1},{2,3},{32,33},{34,35},{64,65},{66,67},{96,97},{98,99},{128,1... | collective-permute-start | bytes 786440 | tf_op jit(solution)/shard_map/ppermute | solution.py:283
  58.0 15.5 %collective-permute-start.6 = (f32[1,64,512]{2,1,0:T(8,128)S(1)}, f32[1,64,512]{2,1,0:T(8,128)S(1)}, u32[]{:S(2)}, u32[]{:S(2)}) collective-permute-start(f32[1,64,512]{2,1,0:T(8,128)S(1)} %broadcast_select_fusion.10), channel_id=1, source_target_pairs={{0,16},{1,17},{2,18},{3,19},{32,48},{33,49},{34,50},{35,51},{64,80... | collective-permute-start | bytes 393224 | tf_op jit(solution)/shard_map/ppermute | solution.py:283
  59.3 25.4 %collective-permute-start.12 = (f32[256,512]{1,0:T(8,128)S(1)}, f32[256,512]{1,0:T(8,128)}, u32[]{:S(2)}, u32[]{:S(2)}) collective-permute-start(f32[256,512]{1,0:T(8,128)S(1)} %get-tuple-element.53), channel_id=1, source_target_pairs={{0,12},{1,13},{32,44},{33,45},{64,76},{65,77},{96,108},{97,109},{1... | collective-permute-start | bytes 1572872 | tf_op jit(solution)/shard_map/ppermute | solution.py:283
  61.4 31.5 %collective-permute-start.13 = (f32[256,512]{1,0:T(8,128)S(1)}, f32[256,512]{1,0:T(8,128)}, u32[]{:S(2)}, u32[]{:S(2)}) collective-permute-start(f32[256,512]{1,0:T(8,128)S(1)} %get-tuple-element.52), channel_id=1, source_target_pairs={{0,16},{1,17},{32,48},{33,49},{64,80},{65,81},{96,112},{97,113},{1... | collective-permute-start | bytes 1572872 | tf_op jit(solution)/shard_map/ppermute | solution.py:283
  70.8 22.1 %collective-permute-start.14 = (f32[256,512]{1,0:T(8,128)S(1)}, f32[256,512]{1,0:T(8,128)}, u32[]{:S(2)}, u32[]{:S(2)}) collective-permute-start(f32[256,512]{1,0:T(8,128)S(1)} %get-tuple-element.51), channel_id=1, source_target_pairs={{0,20},{1,21},{32,52},{33,53},{64,84},{65,85},{96,116},{97,117},{1... | collective-permute-start | bytes 1572872 | tf_op jit(solution)/shard_map/ppermute | solution.py:283
  73.6 20.9 %collective-permute-start.15 = (f32[256,512]{1,0:T(8,128)S(1)}, f32[256,512]{1,0:T(8,128)}, u32[]{:S(2)}, u32[]{:S(2)}) collective-permute-start(f32[256,512]{1,0:T(8,128)S(1)} %get-tuple-element.50), channel_id=1, source_target_pairs={{0,24},{1,25},{32,56},{33,57},{64,88},{65,89},{96,120},{97,121},{1... | collective-permute-start | bytes 1572872 | tf_op jit(solution)/shard_map/ppermute | solution.py:283
  76.3 23.8 %collective-permute-start.16 = (f32[256,512]{1,0:T(8,128)S(1)}, f32[256,512]{1,0:T(8,128)}, u32[]{:S(2)}, u32[]{:S(2)}) collective-permute-start(f32[256,512]{1,0:T(8,128)S(1)} %get-tuple-element.49), channel_id=1, source_target_pairs={{0,28},{1,29},{32,60},{33,61},{64,92},{65,93},{96,124},{97,125},{1... | collective-permute-start | bytes 1572872 | tf_op jit(solution)/shard_map/ppermute | solution.py:283
  113.6 9.9 %collective-permute-start.26 = (f32[2,64,512]{2,1,0:T(8,128)S(1)}, f32[2,64,512]{2,1,0:T(8,128)S(1)}, u32[]{:S(2)}, u32[]{:S(2)}) collective-permute-start(f32[2,64,512]{2,1,0:T(8,128)S(1)} %broadcast_select_fusion.6), channel_id=1, source_target_pairs={{0,16},{1,17},{2,18},{3,19},{32,48},{33,49},{34,50},{35,51},{64,80... | collective-permute-start | bytes 786440 | tf_op jit(solution)/shard_map/ppermute | solution.py:283
  123.6 9.8 %collective-permute-start.27 = (f32[2,64,512]{2,1,0:T(8,128)S(1)}, f32[2,64,512]{2,1,0:T(8,128)S(1)}, u32[]{:S(2)}, u32[]{:S(2)}) collective-permute-start(f32[2,64,512]{2,1,0:T(8,128)S(1)} %broadcast_select_fusion.2), channel_id=1, source_target_pairs={{0,8},{1,9},{2,10},{3,11},{16,24},{17,25},{18,26},{19,27},{32,40},... | collective-permute-start | bytes 786440 | tf_op jit(solution)/shard_map/ppermute | solution.py:283
  125.0 10.5 %collective-permute-start.22 = (f32[1,64,512]{2,1,0:T(8,128)S(1)}, f32[1,64,512]{2,1,0:T(8,128)S(1)}, u32[]{:S(2)}, u32[]{:S(2)}) collective-permute-start(f32[1,64,512]{2,1,0:T(8,128)S(1)} %broadcast_select_fusion.8), channel_id=1, source_target_pairs={{0,64},{1,65},{2,66},{3,67},{4,68},{5,69},{6,70},{7,71},{8,72},{9,... | collective-permute-start | bytes 393224 | tf_op jit(solution)/shard_map/ppermute | solution.py:283
  133.5 9.2 %collective-permute-start.28 = (f32[2,64,512]{2,1,0:T(8,128)S(1)}, f32[2,64,512]{2,1,0:T(8,128)S(1)}, u32[]{:S(2)}, u32[]{:S(2)}) collective-permute-start(f32[2,64,512]{2,1,0:T(8,128)S(1)} %broadcast_select_fusion.3), channel_id=1, source_target_pairs={{0,4},{1,5},{2,6},{3,7},{8,12},{9,13},{10,14},{11,15},{16,20},{17,... | collective-permute-start | bytes 786440 | tf_op jit(solution)/shard_map/ppermute | solution.py:283
  136.0 23.1 %collective-permute-start.25 = (f32[4,1,64,512]{3,2,1,0:T(8,128)S(1)}, f32[4,1,64,512]{3,2,1,0:T(8,128)}, u32[]{:S(2)}, u32[]{:S(2)}) collective-permute-start(f32[4,1,64,512]{3,2,1,0:T(8,128)S(1)} %pad_maximum_fusion.1.mine_ref), channel_id=1, source_target_pairs={{0,32},{1,33},{2,34},{3,35},{4,36},{5,37},{6,38},{7,39},{8,40},{9,... | collective-permute-start | bytes 1572872 | tf_op jit(solution)/shard_map/ppermute | solution.py:283
  136.1 10.6 %collective-permute-start.29 = (f32[2,64,512]{2,1,0:T(8,128)S(1)}, f32[2,64,512]{2,1,0:T(8,128)S(1)}, u32[]{:S(2)}, u32[]{:S(2)}) collective-permute-start(f32[2,64,512]{2,1,0:T(8,128)S(1)} %copy-done.1), channel_id=1, source_target_pairs={{0,0},{1,32},{2,64},{3,96},{4,128},{5,160},{6,192},{7,224},{32,1},... | collective-permute-start | bytes 786440 | tf_op jit(solution)/shard_map/ppermute | solution.py:283
  146.8 34.0 %collective-permute-start.30 = (f32[4,64,512]{2,1,0:T(8,128)S(1)}, f32[4,64,512]{2,1,0:T(8,128)S(1)}, u32[]{:S(2)}, u32[]{:S(2)}) collective-permute-start(f32[4,64,512]{2,1,0:T(8,128)S(1)} %pad_maximum_fusion.2), channel_id=1, source_target_pairs={{0,64},{1,65},{2,66},{3,67},{4,68},{5,69},{6,70},{7,71},{8,72},{9,... | collective-permute-start | bytes 1572872 | tf_op jit(solution)/shard_map/ppermute | solution.py:283
  155.4 25.4 %collective-permute-start.31 = (f32[4,64,512]{2,1,0:T(8,128)S(1)}, f32[4,64,512]{2,1,0:T(8,128)S(1)}, u32[]{:S(2)}, u32[]{:S(2)}) collective-permute-start(f32[4,64,512]{2,1,0:T(8,128)S(1)} %pad_maximum_fusion.2), channel_id=1, source_target_pairs={{0,128},{1,129},{2,130},{3,131},{4,132},{5,133},{6,134},{7,135},{8... | collective-permute-start | bytes 1572872 | tf_op jit(solution)/shard_map/ppermute | solution.py:283
  156.6 24.3 %collective-permute-start.32 = (f32[4,64,512]{2,1,0:T(8,128)S(1)}, f32[4,64,512]{2,1,0:T(8,128)S(1)}, u32[]{:S(2)}, u32[]{:S(2)}) collective-permute-start(f32[4,64,512]{2,1,0:T(8,128)S(1)} %pad_maximum_fusion.2), channel_id=1, source_target_pairs={{0,192},{1,193},{2,194},{3,195},{4,196},{5,197},{6,198},{7,199},{8... | collective-permute-start | bytes 1572872 | tf_op jit(solution)/shard_map/ppermute | solution.py:283
  (17 other events, 115.4 us)
Sparse Core Ops, SparseCore 0:
  112.3 99.3 all-gather.2
